TPU v7x, 32 devices: a whole 2x2x4 slice. The times are simulated.
32 devices in a mesh: grp: 2 (over y), lat: 4 (over z), freq: 4 (over x, core).
Axes of the slice: x: 2, y: 2, z: 4, core: 2. Of those that a mesh axis runs over, the one named last changes fastest.
Arguments:
- source_field: bfloat16 [4, 4, 2304, 512], P('grp', 'freq', 'lat'), parts along dimension 0, may hold values from -6 to 6
- data_field: bfloat16 [4, 4, 2304, 512], P('grp', 'freq', 'lat'), parts along dimension 0, may hold values from -6 to 6
- propagator: bfloat16 [4, 2, 4, 2304, 1152], P('grp', None, 'freq', 'lat'), parts along dimension 0, may hold values from -0.125 to 0.125
- band_start: int32 [4, 4], P('grp', 'lat'), parts along dimension 0, may hold values from 0 to 576, as said below
- freq_slot: int32 [4], P('freq'), may hold values from 0 to 63, as said below
Outputs:
- reflectivity: bfloat16 [4, 2304, 576], P('grp', 'lat'), parts along dimension 0
- source_out: bfloat16 [4, 4, 2304, 512], P('grp', 'freq', 'lat'), parts along dimension 0
- data_out: bfloat16 [4, 4, 2304, 512], P('grp', 'freq', 'lat'), parts along dimension 0
There are 2 independent parts, one for each index of `grp`. A program takes and returns all parts, laid end to end along the dimension named above; an argument that names none is the same for every part. Nothing has to cross between parts.
Inputs may be any that keep to these rules, and one draw needn't show every extreme that they name: `band_start`: every level has one tile whose band starts at 0 and one whose band starts at 576. `freq_slot`: the values are distinct, each block of 16 consecutive values holds exactly one, and both the least and the largest value occur.
All inputs are finite; a program needn't handle non-finite values.
Results may differ from a plain program's by a relative error of at most 0.0092.
Values may be sent and summed in bfloat16 or wider, within the bound.
A program may use at most 64 MiB of HBM per device.

v0:
```python
import math

import jax
import jax.numpy as jnp
from jax import lax
from jax.sharding import PartitionSpec as P

LEVELS = 2


def extended_2(cells, sides, width):
    for axis, dim in sides:
        count = lax.axis_size(axis)
        ends = count - 1
        head = lax.slice_in_dim(cells, 0, width, axis=dim)
        tail = lax.slice_in_dim(cells, cells.shape[dim] - width, cells.shape[dim], axis=dim)
        cells = jnp.concatenate(
            [
                lax.ppermute(tail, axis, [(i, (i + 1) % count) for i in range(ends)]),
                cells,
                lax.ppermute(head, axis, [((i + 1) % count, i) for i in range(ends)]),
            ],
            axis=dim,
        )
    return cells


def per_device(source_field, data_field, propagator, band_start, freq_slot):
    tile_len = source_field.shape[2]
    shot_count = source_field.shape[3]
    band_len = propagator.shape[4]
    freq_total = source_field.shape[1] * lax.axis_size("freq")
    weight = (freq_slot.astype(jnp.float32) + 1.0) / (16.0 * freq_total)
    norm = 1.0 / math.sqrt(freq_total * shot_count)
    source, record = (source_field, data_field)
    levels_out = []
    for level in range(LEVELS):
        stacked = jnp.stack([source, record])
        extended = extended_2(stacked, (("lat", 3),), tile_len)
        window = lax.dynamic_slice_in_dim(extended, band_start[level, 0], band_len, 3)
        rows_r = propagator[level, 0]
        rows_i = propagator[level, 1]
        out_r = jnp.einsum(
            "fxb,nfbs->nfxs", rows_r, window[:, 0], preferred_element_type=jnp.float32
        ) - jnp.einsum("fxb,nfbs->nfxs", rows_i, window[:, 1], preferred_element_type=jnp.float32)
        out_i = jnp.einsum(
            "fxb,nfbs->nfxs", rows_r, window[:, 1], preferred_element_type=jnp.float32
        ) + jnp.einsum("fxb,nfbs->nfxs", rows_i, window[:, 0], preferred_element_type=jnp.float32)
        both = jnp.stack([out_r, out_i], 1).astype(jnp.bfloat16)
        upper, lower = (both[0], both[1])
        per_freq = jnp.einsum("cfxs,cfys->fxy", upper, lower, preferred_element_type=jnp.float32)
        share = lax.psum_scatter(
            jnp.einsum("f,fxy->xy", weight, per_freq) * norm,
            "freq",
            scatter_dimension=0,
            tiled=True,
        )
        saturated = lax.all_gather(jnp.tanh(share).astype(jnp.bfloat16), "freq", axis=0, tiled=True)
        scattered = jnp.einsum(
            "xy,cfys->cfxs", saturated, upper, preferred_element_type=jnp.float32
        ) / math.sqrt(tile_len)
        source = (upper.astype(jnp.float32) + scattered).astype(jnp.bfloat16)
        record = lower
        levels_out.append(saturated)
    return (jnp.stack(levels_out), source, record)


def solution(mesh):
    return jax.shard_map(
        per_device,
        mesh=mesh,
        in_specs=(
            P("grp", "freq", "lat", None),
            P("grp", "freq", "lat", None),
            P("grp", None, "freq", "lat", None),
            P("grp", "lat"),
            P("freq"),
        ),
        out_specs=(
            P("grp", "lat", None),
            P("grp", "freq", "lat", None),
            P("grp", "freq", "lat", None),
        ),
        check_vma=False,
    )
```

profile of v0, /device:TPU:11, one launch (start us, length us, event | category | flops | bytes accessed | tf_op | source)
XLA Modules:
  0.0 255.4 jit_solution(13698666618811240207)
XLA Ops:
  7.2 3.4 %pad_maximum_fusion = bf16[2,2,1,576,512]{4,3,0,2,1:T(8,128)(2,1)} fusion(bf16[1,2,1,576,512]{4,3,0,2,1:T(8,128)(2,1)} %bitcast.154, bf16[1,2,1,576,512]{4,3,0,2,1:T(8,128)(2,1)} %bitcast.156), kind=kLoop, calls=%fused_computation.18 | loop fusion | flops 1179648 | bytes 4718592 | tf_op jit(solution)/shard_map/stack | solution.py:38
  10.7 2.1 collective-permute-start.1
  12.7 3.2 %collective-permute-start = (bf16[2,2,1,576,512]{4,3,0,2,1:T(8,128)(2,1)}, bf16[2,2,1,576,512]{4,3,0,2,1:T(8,128)(2,1)}, u32[]{:S(2)}, u32[]{:S(2)}) collective-permute-start(bf16[2,2,1,576,512]{4,3,0,2,1:T(8,128)(2,1)} %pad_maximum_fusion), channel_id=1, source_target_pairs={{0,4},{4,8},{8,12},{1,5},{5,9},{9,13},{2,6},{6,10},{10,14},{3,7},{... | collective-permute-start | bytes 7077896 | tf_op jit(solution)/shard_map/ppermute | solution.py:19
  19.1 45.8 %collective-permute-done.1 = bf16[2,2,1,576,512]{4,3,0,2,1:T(8,128)(2,1)} collective-permute-done((bf16[2,2,1,576,512]{4,3,0,2,1:T(8,128)(2,1)}, bf16[2,2,1,576,512]{4,3,0,2,1:T(8,128)(2,1)}, u32[]{:S(2)}, u32[]{:S(2)}) %collective-permute-start.1) | collective-permute-done | bytes 2359328 | tf_op jit(solution)/shard_map/ppermute | solution.py:21
  65.0 1.8 collective-permute-done
  66.8 6.8 %fusion.4 = bf16[2,2,1,1152,512]{4,3,0,2,1:T(8,128)(2,1)S(1)} fusion(s32[]{:T(128)S(6)} %select_n.6, bf16[2,2,1,576,512]{4,3,0,2,1:T(8,128)(2,1)} %collective-permute-done, bf16[1,2,1,576,512]{4,3,0,2,1:T(8,128)(2,1)S(1)} %bitcast.157, bf16[1,2,1,576,512]{4,3,0,2,1:T(8,128)(2,1)S(1)} %bitcast.155, bf16[2,2,1,576,512]{4,3,0,2,1:T(8,128)(2,1)} %collective-permute-done.1), kind=kLoop, calls=%fused_computation.12 | loop fusion | flops 18874368 | bytes 11796484 | tf_op jit(solution)/shard_map/concatenate | solution.py:17
  73.6 3.2 %fusion.10 = f32[2,512,576]{1,2,0:T(8,128)S(1)} fusion(bf16[2,2,1,1152,512]{4,3,0,2,1:T(8,128)(2,1)S(1)} %fusion.4, bf16[2,2,1,576,1152]{4,3,2,1,0:T(8,128)(2,1)} %param.7), kind=kOutput, calls=%fused_computation.34 | convolution fusion | flops 1358954496 | bytes 6045696 | tf_op jit(solution)/shard_map/fxb,nfbs->nfxs/dot_general | solution.py:45
  76.8 1.7 fusion.9
  78.5 1.7 fusion.20
  80.2 1.7 fusion.21
  82.9 2.2 fusion.17
  85.2 30.5 %reduce-scatter.3.cloned.1.call-done = f32[144,576]{1,0:T(8,128)} async-done(((f32[576,576]{1,0:T(8,128)}), f32[144,576]{1,0:T(8,128)}) %reduce-scatter.3.cloned.1.call-update) | async-done | bytes 331792 | tf_op jit(solution)/shard_map/reduce_scatter | solution.py:52
  115.7 1.0 tanh_convert_fusion.1
  116.7 8.8 %all_gather.6 = bf16[576,576]{1,0:T(8,128)(2,1)S(1)} all-gather(bf16[144,576]{1,0:T(8,128)(2,1)S(1)} %tanh_convert_fusion.1), channel_id=1, replica_groups=mesh['grp'=2,'lat'=4,'freq'=4] {'freq'}, dimensions={0}, use_global_device_ids=true | all-gather | bytes 829440 | tf_op jit(solution)/shard_map/all_gather | solution.py:58
  125.6 2.8 %fusion.18 = bf16[1,2,1,576,512]{4,3,0,2,1:T(8,128)(2,1)S(1)} fusion(bf16[576,576]{1,0:T(8,128)(2,1)S(1)} %all_gather.6, bf16[2,1,1,576,512]{4,3,0,2,1:T(8,128)(2,1)} %copy-done.3, bf16[2,1,1,576,512]{4,3,0,2,1:T(8,128)(2,1)} %copy-done.2), kind=kOutput, calls=%fused_computation.45 | convolution fusion | flops 684785664 | bytes 6561792 | tf_op jit(solution)/shard_map/xy,cfys->cfxs/dot_general | solution.py:59
  128.3 1.6 pad_maximum_fusion.1
  130.0 2.2 collective-permute-start.3
  132.1 3.3 %collective-permute-start.2 = (bf16[2,2,1,576,512]{4,3,0,2,1:T(8,128)(2,1)}, bf16[2,2,1,576,512]{4,3,0,2,1:T(8,128)(2,1)}, u32[]{:S(2)}, u32[]{:S(2)}) collective-permute-start(bf16[2,2,1,576,512]{4,3,0,2,1:T(8,128)(2,1)} %pad_maximum_fusion.1), channel_id=1, source_target_pairs={{0,4},{4,8},{8,12},{1,5},{5,9},{9,13},{2,6},{6,10},{10,14},{3,7},{... | collective-permute-start | bytes 7077896 | tf_op jit(solution)/shard_map/ppermute | solution.py:19
  137.1 47.7 %collective-permute-done.3 = bf16[2,2,1,576,512]{4,3,0,2,1:T(8,128)(2,1)} collective-permute-done((bf16[2,2,1,576,512]{4,3,0,2,1:T(8,128)(2,1)}, bf16[2,2,1,576,512]{4,3,0,2,1:T(8,128)(2,1)}, u32[]{:S(2)}, u32[]{:S(2)}) %collective-permute-start.3) | collective-permute-done | bytes 2359328 | tf_op jit(solution)/shard_map/ppermute | solution.py:21
  184.8 1.9 collective-permute-done.2
  186.7 6.7 %fusion.1 = bf16[2,2,1,1152,512]{4,3,0,2,1:T(8,128)(2,1)S(1)} fusion(s32[]{:T(128)S(6)} %select_n.7, bf16[2,2,1,576,512]{4,3,0,2,1:T(8,128)(2,1)} %collective-permute-done.2, bf16[1,2,1,576,512]{4,3,0,2,1:T(8,128)(2,1)S(1)} %fusion.18, bf16[1,2,1,576,512]{4,3,0,2,1:T(8,128)(2,1)S(1)} %pad_maximum_fusion.4, bf16[2,2,1,576,512]{4,3,0,2,1:T(8,128)(2,1)} %collective-permute-done.3), kind=kLoop, calls=%fused_computation.9 | loop fusion | flops 18874368 | bytes 11796484 | tf_op jit(solution)/shard_map/concatenate | solution.py:17
  193.5 3.2 %fusion.14 = f32[2,512,576]{1,2,0:T(8,128)S(1)} fusion(bf16[2,2,1,1152,512]{4,3,0,2,1:T(8,128)(2,1)S(1)} %fusion.1, bf16[2,2,1,576,1152]{4,3,2,1,0:T(8,128)(2,1)} %param.7), kind=kOutput, calls=%fused_computation.38 | convolution fusion | flops 1358954496 | bytes 6045696 | tf_op jit(solution)/shard_map/fxb,nfbs->nfxs/dot_general | solution.py:45
  196.6 3.1 %fusion.13 = f32[2,512,576]{1,2,0:T(8,128)S(1)} fusion(bf16[2,2,1,1152,512]{4,3,0,2,1:T(8,128)(2,1)S(1)} %fusion.1, bf16[2,2,1,576,1152]{4,3,2,1,0:T(8,128)(2,1)} %param.7), kind=kOutput, calls=%fused_computation.37 | convolution fusion | flops 1358954496 | bytes 6045696 | tf_op jit(solution)/shard_map/fxb,nfbs->nfxs/dot_general | solution.py:48
  199.8 1.7 fusion.22
  201.5 1.7 fusion.23
  203.2 2.2 fusion.16
  205.5 1.1 fusion.50
  206.6 28.6 %reduce-scatter.5.cloned.1.call-done = f32[144,576]{1,0:T(8,128)} async-done(((f32[576,576]{1,0:T(8,128)}), f32[144,576]{1,0:T(8,128)}) %reduce-scatter.5.cloned.1.call-update) | async-done | bytes 331792 | tf_op jit(solution)/shard_map/reduce_scatter | solution.py:52
  235.2 1.0 tanh_convert_fusion
  236.2 8.8 %all_gather.7 = bf16[576,576]{1,0:T(8,128)(2,1)S(1)} all-gather(bf16[144,576]{1,0:T(8,128)(2,1)S(1)} %tanh_convert_fusion), channel_id=1, replica_groups=mesh['grp'=2,'lat'=4,'freq'=4] {'freq'}, dimensions={0}, use_global_device_ids=true | all-gather | bytes 829440 | tf_op jit(solution)/shard_map/all_gather | solution.py:58
  245.1 2.1 fusion.19
  247.2 1.3 pad_maximum_fusion.2
  (23 shorter events, 1.7 us)
Async XLA Ops:
  7.2 108.5 %reduce-scatter.3.cloned.1.call-start = ((), (), s32[]{:S(2)}) async-start(), calls=%async_computation.2 | async-start | bytes 1843200 | tf_op jit(solution)/shard_map/reduce_scatter | solution.py:52
  7.2 9.4 %copy-start.4 = (s32[2,1]{0,1:T(1,128)S(1)}, s32[2,1]{0,1:T(1,128)}, u32[]{:S(2)}) copy-start(s32[2,1]{0,1:T(1,128)} %param.8) | copy-start | bytes 28
  7.2 59.5 %copy-start = (bf16[2,1,576,512]{3,2,1,0:T(8,128)(2,1)S(1)}, bf16[2,1,576,512]{3,2,1,0:T(8,128)(2,1)}, u32[]{:S(2)}) copy-start(bf16[2,1,576,512]{3,2,1,0:T(8,128)(2,1)} %param.6) | copy-start | bytes 3538948
  7.2 59.5 %copy-start.1 = (bf16[2,1,576,512]{3,2,1,0:T(8,128)(2,1)S(1)}, bf16[2,1,576,512]{3,2,1,0:T(8,128)(2,1)}, u32[]{:S(2)}) copy-start(bf16[2,1,576,512]{3,2,1,0:T(8,128)(2,1)} %param.5) | copy-start | bytes 3538948
  10.7 54.3 %collective-permute-start.1 = (bf16[2,2,1,576,512]{4,3,0,2,1:T(8,128)(2,1)}, bf16[2,2,1,576,512]{4,3,0,2,1:T(8,128)(2,1)}, u32[]{:S(2)}, u32[]{:S(2)}) collective-permute-start(bf16[2,2,1,576,512]{4,3,0,2,1:T(8,128)(2,1)} %pad_maximum_fusion), channel_id=1, source_target_pairs={{4,0},{8,4},{12,8},{5,1},{9,5},{13,9},{6,2},{10,6},{14,10},{7,3},{... | collective-permute-start | bytes 7077896 | tf_op jit(solution)/shard_map/ppermute | solution.py:21
  12.7 54.0 %collective-permute-start = (bf16[2,2,1,576,512]{4,3,0,2,1:T(8,128)(2,1)}, bf16[2,2,1,576,512]{4,3,0,2,1:T(8,128)(2,1)}, u32[]{:S(2)}, u32[]{:S(2)}) collective-permute-start(bf16[2,2,1,576,512]{4,3,0,2,1:T(8,128)(2,1)} %pad_maximum_fusion), channel_id=1, source_target_pairs={{0,4},{4,8},{8,12},{1,5},{5,9},{9,13},{2,6},{6,10},{10,14},{3,7},{... | collective-permute-start | bytes 7077896 | tf_op jit(solution)/shard_map/ppermute | solution.py:19
  73.6 3.2 %copy-start.5 = (bf16[2,2,1,576,1152]{4,3,2,1,0:T(8,128)(2,1)S(1)}, bf16[2,2,1,576,1152]{4,3,2,1,0:T(8,128)(2,1)}, u32[]{:S(2)}) copy-start(bf16[2,2,1,576,1152]{4,3,2,1,0:T(8,128)(2,1)} %param.7) | copy-start | bytes 15925252
  80.2 1.9 copy-start.2
  81.9 1.0 copy-start.3
  85.2 150.0 %reduce-scatter.5.cloned.1.call-start = ((), (), s32[]{:S(2)}) async-start(), calls=%async_computation.3 | async-start | bytes 1843200 | tf_op jit(solution)/shard_map/reduce_scatter | solution.py:52
  130.0 54.9 %collective-permute-start.3 = (bf16[2,2,1,576,512]{4,3,0,2,1:T(8,128)(2,1)}, bf16[2,2,1,576,512]{4,3,0,2,1:T(8,128)(2,1)}, u32[]{:S(2)}, u32[]{:S(2)}) collective-permute-start(bf16[2,2,1,576,512]{4,3,0,2,1:T(8,128)(2,1)} %pad_maximum_fusion.1), channel_id=1, source_target_pairs={{4,0},{8,4},{12,8},{5,1},{9,5},{13,9},{6,2},{10,6},{14,10},{7,3},{... | collective-permute-start | bytes 7077896 | tf_op jit(solution)/shard_map/ppermute | solution.py:21
  132.1 54.6 %collective-permute-start.2 = (bf16[2,2,1,576,512]{4,3,0,2,1:T(8,128)(2,1)}, bf16[2,2,1,576,512]{4,3,0,2,1:T(8,128)(2,1)}, u32[]{:S(2)}, u32[]{:S(2)}) collective-permute-start(bf16[2,2,1,576,512]{4,3,0,2,1:T(8,128)(2,1)} %pad_maximum_fusion.1), channel_id=1, source_target_pairs={{0,4},{4,8},{8,12},{1,5},{5,9},{9,13},{2,6},{6,10},{10,14},{3,7},{... | collective-permute-start | bytes 7077896 | tf_op jit(solution)/shard_map/ppermute | solution.py:19
  193.4 6.3 %slice-start = ((s8[5308416]{0:T(1024)(128)(4,1)}), s8[4194304]{0:T(1024)(128)(4,1)S(1)}, s32[]{:S(2)}) async-start(s8[5308416]{0:T(1024)(128)(4,1)} %bitcast.160), calls=%async_computation.4 | async-start | bytes 8388608
  196.6 3.1 %slice-start.1 = ((s8[5308416]{0:T(1024)(128)(4,1)}), s8[1114112]{0:T(1024)(128)(4,1)S(1)}, s32[]{:S(2)}) async-start(s8[5308416]{0:T(1024)(128)(4,1)} %bitcast.160), calls=%async_computation.5 | async-start | bytes 2228224
Sparse Core Ops, SparseCore 0:
  85.3 30.3 reduce-scatter.2
  205.6 29.5 reduce-scatter.4
where the time goes:
time: 257 us; the launch traced here: 255 us
  waiting for transfers between devices  156 us (61%)
  matrix products  27.3 us (11%)
  other arithmetic  23.3 us (9%)
  between operations  18.6 us (7%)
  blocking collectives  17.7 us (7%)
  starting transfers between devices  10.8 us (4%)
    ppermute x2, waiting for transfers between devices, extended_2(): lax.ppermute(head, axis, [((i + 1) % count, i) for i in range(ends)])  93.5 us
    reduce_scatter x2, waiting for transfers between devices, per_device(): lax.psum_scatter(jnp.einsum('f,fxy->xy', weight, per_freq) * norm, 'freq'...  59.1 us
    all_gather x2, blocking collectives, per_device(): lax.all_gather(jnp.tanh(share).astype(jnp.bfloat16), 'freq', axis=0, tile...  17.7 us
    concatenate x2, other arithmetic, extended_2(): jnp.concatenate([lax.ppermute(tail, axis, [(i, (i + 1) % count) for i in...  13.5 us
    ppermute x2, starting transfers between devices, extended_2(): lax.ppermute(tail, axis, [(i, (i + 1) % count) for i in range(ends)])  6.5 us
    dot_general x2, matrix products, per_device(): jnp.einsum('fxb,nfbs->nfxs', rows_i, window[:, 1], preferred_element_type...  6.33 us
  transfers between devices with their start and end apart: 6, of which 6 were waited for; matrix products, arithmetic and copies ran while one was open for 1% of the time, Pallas kernels for 0%

commit v1 on v0

v1 whole, which is shorter than its diff:
```python
import math

import jax
import jax.numpy as jnp
from jax import lax
from jax.sharding import PartitionSpec as P

LEVELS = 2


def neighbours(cells, axis):
    count = lax.axis_size(axis)
    ends = count - 1
    from_left = lax.ppermute(cells, axis, [(i, (i + 1) % count) for i in range(ends)])
    from_right = lax.ppermute(cells, axis, [((i + 1) % count, i) for i in range(ends)])
    return from_left, from_right


def advance(rows_r, rows_i, parts, start):
    extended = jnp.concatenate(parts, axis=1)
    window = lax.dynamic_slice_in_dim(extended, start, rows_r.shape[1], 1)

    def dot(a, b):
        return jnp.einsum("xb,bs->xs", a, b, preferred_element_type=jnp.float32)

    out_r = dot(rows_r, window[0]) - dot(rows_i, window[1])
    out_i = dot(rows_r, window[1]) + dot(rows_i, window[0])
    return jnp.stack([out_r, out_i]).astype(jnp.bfloat16)


def per_device(source_field, data_field, propagator, band_start, freq_slot):
    tile_len = source_field.shape[2]
    shot_count = source_field.shape[3]
    freq_total = source_field.shape[1] * lax.axis_size("freq")
    weight = (freq_slot[0].astype(jnp.float32) + 1.0) / (16.0 * freq_total)
    norm = 1.0 / math.sqrt(freq_total * shot_count)
    source, record = (source_field[:, 0], data_field[:, 0])
    record_l, record_r = neighbours(record, "lat")
    source_l, source_r = neighbours(source, "lat")
    source_parts = [source_l, source, source_r]
    levels_out = []
    for level in range(LEVELS):
        last = level == LEVELS - 1
        rows_r = propagator[level, 0, 0]
        rows_i = propagator[level, 1, 0]
        start = band_start[level, 0]
        lower = advance(rows_r, rows_i, [record_l, record, record_r], start)
        upper = advance(rows_r, rows_i, source_parts, start)
        if not last:
            record_l, record_r = neighbours(lower, "lat")
            upper_l, upper_r = neighbours(upper, "lat")
        gram = jnp.einsum("cxs,cys->xy", upper, lower, preferred_element_type=jnp.float32)
        share = lax.psum_scatter(gram * (weight * norm), "freq", scatter_dimension=0, tiled=True)
        share = jnp.tanh(share).astype(jnp.bfloat16)
        if last:
            saturated = lax.all_gather(share, "freq", axis=0, tiled=True)
            tiles, fields = ([saturated], [upper])
        else:
            share_l, share_r = neighbours(share, "lat")
            trio = lax.all_gather(jnp.stack([share_l, share, share_r]), "freq", axis=1, tiled=True)
            tiles, fields = ([trio[0], trio[1], trio[2]], [upper_l, upper, upper_r])
            saturated = trio[1]
        source_parts = [
            (
                field.astype(jnp.float32)
                + jnp.einsum("xy,cys->cxs", tile, field, preferred_element_type=jnp.float32)
                / math.sqrt(tile_len)
            ).astype(jnp.bfloat16)
            for tile, field in zip(tiles, fields)
        ]
        record = lower
        levels_out.append(saturated)
    return (jnp.stack(levels_out), source_parts[0][:, None], record[:, None])


def solution(mesh):
    return jax.shard_map(
        per_device,
        mesh=mesh,
        in_specs=(
            P("grp", "freq", "lat", None),
            P("grp", "freq", "lat", None),
            P("grp", None, "freq", "lat", None),
            P("grp", "lat"),
            P("freq"),
        ),
        out_specs=(
            P("grp", "lat", None),
            P("grp", "freq", "lat", None),
            P("grp", "freq", "lat", None),
        ),
        check_vma=False,
    )
```

time: 257 us -> 217 us (0.84)
  waiting for transfers between devices: 156 us -> 101 us
  starting transfers between devices: 10.8 us -> 27.9 us
  blocking collectives: 17.7 us -> 8.82 us
  matrix products: 27.3 us -> 33.4 us
    ppermute x4 -> x10, waiting for transfers between devices: 97.2 us -> 51.8 us  [the longest x5 32.1 us: neighbours(): lax.ppermute(cells, axis, [(i, (i + 1) % count) for i in range(ends)])]
    ppermute x4 -> x10, starting transfers between devices: 10.7 us -> 27.8 us  [the longest x5 16 us: neighbours(): lax.ppermute(cells, axis, [(i, (i + 1) % count) for i in range(ends)])]
    reduce_scatter x2, waiting for transfers between devices: 59.1 us -> 49.4 us  [per_device(): lax.psum_scatter(gram * (weight * norm), 'freq', scatter_dimension=0, til...]
    all_gather x2 -> x1, blocking collectives: 17.7 us -> 8.82 us  [per_device(): saturated = lax.all_gather(share, 'freq', axis=0, tiled=True)]
    dot_general x12 -> x22, matrix products: 27.3 us -> 33.4 us  [the longest x16 18.1 us: dot(): return jnp.einsum('xb,bs->xs', a, b, preferred_element_type=jnp.float32)]
    concatenate x2 -> x4, other arithmetic: 13.5 us -> 15 us  [advance(): extended = jnp.concatenate(parts, axis=1)]
    another operation x4 -> x6, other arithmetic: 6.51 us -> 5.85 us  [the longest x3 2.58 us: advance(): return jnp.stack([out_r, out_i]).astype(jnp.bfloat16)]
  transfers between devices with their start and end apart: 6 -> 13, of which waited for: 6 -> 9; matrix products, arithmetic and copies ran while one was open for 1% -> 14% of each run, Pallas kernels for 0% -> 0%
where the time goes in v1:
time: 217 us; the launch traced here: 215 us
  waiting for transfers between devices  101 us (47%)
  matrix products  33.4 us (15%)
  starting transfers between devices  27.9 us (13%)
  other arithmetic  22.9 us (11%)
  between operations  18.7 us (9%)
  blocking collectives  8.82 us (4%)
  local copies, waits for them, and re-layouts  2.2 us (1%)
    reduce_scatter x2, waiting for transfers between devices, per_device(): lax.psum_scatter(gram * (weight * norm), 'freq', scatter_dimension=0, til...  49.4 us
    ppermute x5, waiting for transfers between devices, neighbours(): lax.ppermute(cells, axis, [(i, (i + 1) % count) for i in range(ends)])  32.1 us
    ppermute x5, waiting for transfers between devices, neighbours(): lax.ppermute(cells, axis, [((i + 1) % count, i) for i in range(ends)])  19.7 us
    dot_general x16, matrix products, dot(): return jnp.einsum('xb,bs->xs', a, b, preferred_element_type=jnp.float32)  18.1 us
    ppermute x5, starting transfers between devices, neighbours(): lax.ppermute(cells, axis, [(i, (i + 1) % count) for i in range(ends)])  16 us
    concatenate x4, other arithmetic, advance(): extended = jnp.concatenate(parts, axis=1)  15 us
    ppermute x5, starting transfers between devices, neighbours(): lax.ppermute(cells, axis, [((i + 1) % count, i) for i in range(ends)])  11.8 us
    dot_general x4, matrix products, per_device(): jnp.einsum('xy,cys->cxs', tile, field, preferred_element_type=jnp.float32)  10.8 us
  transfers between devices with their start and end apart: 13, of which 9 were waited for; matrix products, arithmetic and copies ran while one was open for 14% of the time, Pallas kernels for 0%

profile of v1, /device:TPU:11, one launch (start us, length us, event | category | flops | bytes accessed | tf_op | source)
XLA Modules:
  0.0 215.1 jit_solution(9622144607331494661)
XLA Ops:
  7.2 3.2 %collective-permute-start = (bf16[2,576,512]{2,1,0:T(8,128)(2,1)}, bf16[2,576,512]{2,1,0:T(8,128)(2,1)S(1)}, u32[]{:S(2)}, u32[]{:S(2)}) collective-permute-start(bf16[2,576,512]{2,1,0:T(8,128)(2,1)} %bitcast.184), channel_id=1, source_target_pairs={{0,4},{4,8},{8,12},{1,5},{5,9},{9,13},{2,6},{6,10},{10,14},{3,7},{... | collective-permute-start | bytes 3538952 | tf_op jit(solution)/shard_map/ppermute | solution.py:14
  10.4 2.2 %collective-permute-start.1 = (bf16[2,576,512]{2,1,0:T(8,128)(2,1)}, bf16[2,576,512]{2,1,0:T(8,128)(2,1)}, u32[]{:S(2)}, u32[]{:S(2)}) collective-permute-start(bf16[2,576,512]{2,1,0:T(8,128)(2,1)} %bitcast.185), channel_id=1, source_target_pairs={{4,0},{8,4},{12,8},{5,1},{9,5},{13,9},{6,2},{10,6},{14,10},{7,3},{... | collective-permute-start | bytes 3538952 | tf_op jit(solution)/shard_map/ppermute | solution.py:15
  12.6 3.1 %collective-permute-start.2 = (bf16[2,576,512]{2,1,0:T(8,128)(2,1)}, bf16[2,576,512]{2,1,0:T(8,128)(2,1)S(1)}, u32[]{:S(2)}, u32[]{:S(2)}) collective-permute-start(bf16[2,576,512]{2,1,0:T(8,128)(2,1)} %bitcast.187), channel_id=1, source_target_pairs={{0,4},{4,8},{8,12},{1,5},{5,9},{9,13},{2,6},{6,10},{10,14},{3,7},{... | collective-permute-start | bytes 3538952 | tf_op jit(solution)/shard_map/ppermute | solution.py:14
  15.7 2.2 %collective-permute-start.3 = (bf16[2,576,512]{2,1,0:T(8,128)(2,1)}, bf16[2,576,512]{2,1,0:T(8,128)(2,1)S(1)}, u32[]{:S(2)}, u32[]{:S(2)}) collective-permute-start(bf16[2,576,512]{2,1,0:T(8,128)(2,1)} %bitcast.188), channel_id=1, source_target_pairs={{4,0},{8,4},{12,8},{5,1},{9,5},{13,9},{6,2},{10,6},{14,10},{7,3},{... | collective-permute-start | bytes 3538952 | tf_op jit(solution)/shard_map/ppermute | solution.py:15
  21.9 14.4 %collective-permute-done = bf16[2,576,512]{2,1,0:T(8,128)(2,1)S(1)} collective-permute-done((bf16[2,576,512]{2,1,0:T(8,128)(2,1)}, bf16[2,576,512]{2,1,0:T(8,128)(2,1)S(1)}, u32[]{:S(2)}, u32[]{:S(2)}) %collective-permute-start) | collective-permute-done | bytes 1179680 | tf_op jit(solution)/shard_map/ppermute | solution.py:14
  36.3 2.9 %collective-permute-done.1 = bf16[2,576,512]{2,1,0:T(8,128)(2,1)} collective-permute-done((bf16[2,576,512]{2,1,0:T(8,128)(2,1)}, bf16[2,576,512]{2,1,0:T(8,128)(2,1)}, u32[]{:S(2)}, u32[]{:S(2)}) %collective-permute-start.1) | collective-permute-done | bytes 1179680 | tf_op jit(solution)/shard_map/ppermute | solution.py:15
  39.2 3.7 %fusion.8 = bf16[2,1152,512]{2,1,0:T(8,128)(2,1)S(1)} fusion(s32[]{:T(128)S(6)} %select_n.8, bf16[2,576,512]{2,1,0:T(8,128)(2,1)S(1)} %collective-permute-done, bf16[2,576,512]{2,1,0:T(8,128)(2,1)} %bitcast.186, bf16[2,576,512]{2,1,0:T(8,128)(2,1)} %collective-permute-done.1), kind=kLoop, calls=%fused_computation.21 | loop fusion | flops 7077888 | bytes 5898244 | tf_op jit(solution)/shard_map/concatenate | solution.py:20
  44.8 16.7 %collective-permute-done.2 = bf16[2,576,512]{2,1,0:T(8,128)(2,1)S(1)} collective-permute-done((bf16[2,576,512]{2,1,0:T(8,128)(2,1)}, bf16[2,576,512]{2,1,0:T(8,128)(2,1)S(1)}, u32[]{:S(2)}, u32[]{:S(2)}) %collective-permute-start.2) | collective-permute-done | bytes 1179680 | tf_op jit(solution)/shard_map/ppermute | solution.py:14
  61.4 2.9 %collective-permute-done.3 = bf16[2,576,512]{2,1,0:T(8,128)(2,1)S(1)} collective-permute-done((bf16[2,576,512]{2,1,0:T(8,128)(2,1)}, bf16[2,576,512]{2,1,0:T(8,128)(2,1)S(1)}, u32[]{:S(2)}, u32[]{:S(2)}) %collective-permute-start.3) | collective-permute-done | bytes 1179680 | tf_op jit(solution)/shard_map/ppermute | solution.py:15
  64.3 3.5 %fusion.6 = bf16[2,1152,512]{2,1,0:T(8,128)(2,1)S(1)} fusion(s32[]{:T(128)S(6)} %select_n.8, bf16[2,576,512]{2,1,0:T(8,128)(2,1)S(1)} %collective-permute-done.2, bf16[2,576,512]{2,1,0:T(8,128)(2,1)S(1)} %bitcast.189, bf16[2,576,512]{2,1,0:T(8,128)(2,1)S(1)} %collective-permute-done.3), kind=kLoop, calls=%fused_computation.19 | loop fusion | flops 7077888 | bytes 5898244 | tf_op jit(solution)/shard_map/concatenate | solution.py:20
  73.5 2.2 %bitcast_multiply_fusion.1 = f32[576,576]{1,0:T(8,128)} fusion(f32[]{:T(128)} %bitcast.18, bf16[1,576,512]{2,1,0:T(8,128)(2,1)S(1)} %fusion.68, bf16[1,576,512]{2,1,0:T(8,128)(2,1)S(1)} %fusion.71, bf16[1,576,512]{2,1,0:T(8,128)(2,1)S(1)} %fusion.74, bf16[1,576,512]{2,1,0:T(8,128)(2,1)S(1)} %fusion.77), kind=kOutput, calls=%fused_computation.32 | convolution fusion | flops 680988672 | bytes 3686404 | tf_op jit(solution)/shard_map/cxs,cys->xy/dot_general | solution.py:52
  75.9 3.2 %collective-permute-start.8 = (bf16[2,576,512]{2,1,0:T(8,128)(2,1)S(1)}, bf16[2,576,512]{2,1,0:T(8,128)(2,1)}, u32[]{:S(2)}, u32[]{:S(2)}) collective-permute-start(bf16[2,576,512]{2,1,0:T(8,128)(2,1)S(1)} %pad_maximum_fusion.2), channel_id=1, source_target_pairs={{0,4},{4,8},{8,12},{1,5},{5,9},{9,13},{2,6},{6,10},{10,14},{3,7},{... | collective-permute-start | bytes 3538952 | tf_op jit(solution)/shard_map/ppermute | solution.py:14
  79.1 3.1 %collective-permute-start.9 = (bf16[2,576,512]{2,1,0:T(8,128)(2,1)S(1)}, bf16[2,576,512]{2,1,0:T(8,128)(2,1)}, u32[]{:S(2)}, u32[]{:S(2)}) collective-permute-start(bf16[2,576,512]{2,1,0:T(8,128)(2,1)S(1)} %pad_maximum_fusion.2), channel_id=1, source_target_pairs={{4,0},{8,4},{12,8},{5,1},{9,5},{13,9},{6,2},{10,6},{14,10},{7,3},{... | collective-permute-start | bytes 3538952 | tf_op jit(solution)/shard_map/ppermute | solution.py:15
  82.2 21.6 %reduce-scatter.3.cloned.1.call-done = f32[144,576]{1,0:T(8,128)} async-done(((f32[576,576]{1,0:T(8,128)}), f32[144,576]{1,0:T(8,128)}) %reduce-scatter.3.cloned.1.call-update) | async-done | bytes 331792 | tf_op jit(solution)/shard_map/reduce_scatter | solution.py:53
  104.9 3.1 %collective-permute-start.4 = (bf16[144,576]{1,0:T(8,128)(2,1)S(1)}, bf16[144,576]{1,0:T(8,128)(2,1)S(1)}, u32[]{:S(2)}, u32[]{:S(2)}) collective-permute-start(bf16[144,576]{1,0:T(8,128)(2,1)S(1)} %tanh_convert_fusion.1), channel_id=1, source_target_pairs={{0,4},{4,8},{8,12},{1,5},{5,9},{9,13},{2,6},{6,10},{10,14},{3,7},{... | collective-permute-start | bytes 497672 | tf_op jit(solution)/shard_map/ppermute | solution.py:14
  108.0 2.2 %collective-permute-start.5 = (bf16[144,576]{1,0:T(8,128)(2,1)S(1)}, bf16[144,576]{1,0:T(8,128)(2,1)S(1)}, u32[]{:S(2)}, u32[]{:S(2)}) collective-permute-start(bf16[144,576]{1,0:T(8,128)(2,1)S(1)} %tanh_convert_fusion.1), channel_id=1, source_target_pairs={{4,0},{8,4},{12,8},{5,1},{9,5},{13,9},{6,2},{10,6},{14,10},{7,3},{... | collective-permute-start | bytes 497672 | tf_op jit(solution)/shard_map/ppermute | solution.py:15
  112.3 2.8 %collective-permute-done.5 = bf16[144,576]{1,0:T(8,128)(2,1)S(1)} collective-permute-done((bf16[144,576]{1,0:T(8,128)(2,1)S(1)}, bf16[144,576]{1,0:T(8,128)(2,1)S(1)}, u32[]{:S(2)}, u32[]{:S(2)}) %collective-permute-start.5) | collective-permute-done | bytes 165920 | tf_op jit(solution)/shard_map/ppermute | solution.py:15
  119.4 2.1 collective-permute-start.7
  121.5 3.3 %collective-permute-start.6 = (bf16[2,576,512]{2,1,0:T(8,128)(2,1)S(1)}, bf16[2,576,512]{2,1,0:T(8,128)(2,1)}, u32[]{:S(2)}, u32[]{:S(2)}) collective-permute-start(bf16[2,576,512]{2,1,0:T(8,128)(2,1)S(1)} %pad_maximum_fusion.1), channel_id=1, source_target_pairs={{0,4},{4,8},{8,12},{1,5},{5,9},{9,13},{2,6},{6,10},{10,14},{3,7},{... | collective-permute-start | bytes 3538952 | tf_op jit(solution)/shard_map/ppermute | solution.py:14
  124.9 4.2 %fusion.1 = bf16[2,1152,512]{2,1,0:T(8,128)(2,1)S(1)} fusion(s32[]{:T(128)S(6)} %select_n.9, bf16[2,576,512]{2,1,0:T(8,128)(2,1)} %collective-permute-done.8, bf16[1,576,512]{2,1,0:T(8,128)(2,1)S(1)} %fusion.71, bf16[1,576,512]{2,1,0:T(8,128)(2,1)S(1)} %fusion.68, bf16[2,576,512]{2,1,0:T(8,128)(2,1)} %collective-permute-done.9), kind=kLoop, calls=%fused_computation.14 | loop fusion | flops 9437184 | bytes 5898244 | tf_op jit(solution)/shard_map/concatenate | solution.py:20
  129.1 2.3 %fusion.16 = f32[512,576]{0,1:T(8,128)S(1)} fusion(bf16[2,1152,512]{2,1,0:T(8,128)(2,1)S(1)} %fusion.1, bf16[2,2,1,576,1152]{4,3,2,1,0:T(8,128)(2,1)} %param.7), kind=kOutput, calls=%fused_computation.44 | convolution fusion | flops 679477248 | bytes 3686400 | tf_op jit(solution)/shard_map/xb,bs->xs/dot_general | solution.py:24
  131.5 1.7 fusion.56
  134.2 1.7 fusion.59
  135.9 11.1 %collective-permute-done.7 = bf16[2,576,512]{2,1,0:T(8,128)(2,1)} collective-permute-done((bf16[2,576,512]{2,1,0:T(8,128)(2,1)S(1)}, bf16[2,576,512]{2,1,0:T(8,128)(2,1)}, u32[]{:S(2)}, u32[]{:S(2)}) %collective-permute-start.7) | collective-permute-done | bytes 1179680 | tf_op jit(solution)/shard_map/ppermute | solution.py:15
  147.0 3.1 %fusion.10 = bf16[2,576,512]{2,1,0:T(8,128)(2,1)S(1)} fusion(bf16[2,576,512]{2,1,0:T(8,128)(2,1)} %collective-permute-done.7, bf16[3,576,576]{2,1,0:T(8,128)(2,1)} %all-gather.2.cloned.1.call-done), kind=kOutput, calls=%fused_computation.25 | convolution fusion | flops 681836544 | bytes 4276224 | tf_op jit(solution)/shard_map/xy,cys->cxs/dot_general | solution.py:66
  150.1 2.8 %fusion.11 = bf16[2,576,512]{2,1,0:T(8,128)(2,1)S(1)} fusion(bf16[3,576,576]{2,1,0:T(8,128)(2,1)S(1)} %copy-done, bf16[1,576,512]{2,1,0:T(8,128)(2,1)} %copy-done.2, bf16[1,576,512]{2,1,0:T(8,128)(2,1)} %copy-done.3), kind=kOutput, calls=%fused_computation.27 | convolution fusion | flops 684785664 | bytes 4276224 | tf_op jit(solution)/shard_map/xy,cys->cxs/dot_general | solution.py:66
  152.9 2.8 %fusion.12 = bf16[2,576,512]{2,1,0:T(8,128)(2,1)S(1)} fusion(bf16[2,576,512]{2,1,0:T(8,128)(2,1)} %collective-permute-done.6, bf16[3,576,576]{2,1,0:T(8,128)(2,1)S(1)} %copy-done), kind=kOutput, calls=%fused_computation.29 | convolution fusion | flops 681836544 | bytes 4276224 | tf_op jit(solution)/shard_map/xy,cys->cxs/dot_general | solution.py:66
  155.7 3.5 %fusion.4 = bf16[2,1152,512]{2,1,0:T(8,128)(2,1)S(1)} fusion(s32[]{:T(128)S(6)} %select_n.9, bf16[2,576,512]{2,1,0:T(8,128)(2,1)S(1)} %fusion.12, bf16[2,576,512]{2,1,0:T(8,128)(2,1)S(1)} %fusion.11, bf16[2,576,512]{2,1,0:T(8,128)(2,1)S(1)} %fusion.10), kind=kLoop, calls=%fused_computation.17 | loop fusion | flops 7077888 | bytes 5898244 | tf_op jit(solution)/shard_map/concatenate | solution.py:20
  164.1 2.2 %bitcast_multiply_fusion = f32[576,576]{1,0:T(8,128)} fusion(bf16[1,576,512]{2,1,0:T(8,128)(2,1)S(1)} %bitcast.192, bf16[1,576,512]{2,1,0:T(8,128)(2,1)S(1)} %bitcast.190, bf16[1,576,512]{2,1,0:T(8,128)(2,1)S(1)} %fusion.62, bf16[1,576,512]{2,1,0:T(8,128)(2,1)S(1)} %fusion.65, f32[]{:T(128)} %bitcast.18), kind=kOutput, calls=%fused_computation.31 | convolution fusion | flops 680988672 | bytes 3686404 | tf_op jit(solution)/shard_map/cxs,cys->xy/dot_general | solution.py:52
  167.5 27.8 %reduce-scatter.5.cloned.1.call-done = f32[144,576]{1,0:T(8,128)} async-done(((f32[576,576]{1,0:T(8,128)}), f32[144,576]{1,0:T(8,128)}) %reduce-scatter.5.cloned.1.call-update) | async-done | bytes 331792 | tf_op jit(solution)/shard_map/reduce_scatter | solution.py:53
  196.3 8.8 %all_gather.7 = bf16[576,576]{1,0:T(8,128)(2,1)S(1)} all-gather(bf16[144,576]{1,0:T(8,128)(2,1)S(1)} %tanh_convert_fusion), channel_id=1, replica_groups=mesh['grp'=2,'lat'=4,'freq'=4] {'freq'}, dimensions={0}, use_global_device_ids=true | all-gather | bytes 829440 | tf_op jit(solution)/shard_map/all_gather | solution.py:56
  205.1 2.1 fusion.13
  (67 shorter events, 23.6 us)
Async XLA Ops:
  7.2 96.7 %reduce-scatter.3.cloned.1.call-start = ((), (), s32[]{:S(2)}) async-start(), calls=%async_computation.2 | async-start | bytes 1843200 | tf_op jit(solution)/shard_map/reduce_scatter | solution.py:53
  7.2 29.0 %collective-permute-start = (bf16[2,576,512]{2,1,0:T(8,128)(2,1)}, bf16[2,576,512]{2,1,0:T(8,128)(2,1)S(1)}, u32[]{:S(2)}, u32[]{:S(2)}) collective-permute-start(bf16[2,576,512]{2,1,0:T(8,128)(2,1)} %bitcast.184), channel_id=1, source_target_pairs={{0,4},{4,8},{8,12},{1,5},{5,9},{9,13},{2,6},{6,10},{10,14},{3,7},{... | collective-permute-start | bytes 3538952 | tf_op jit(solution)/shard_map/ppermute | solution.py:14
  10.4 28.7 %collective-permute-start.1 = (bf16[2,576,512]{2,1,0:T(8,128)(2,1)}, bf16[2,576,512]{2,1,0:T(8,128)(2,1)}, u32[]{:S(2)}, u32[]{:S(2)}) collective-permute-start(bf16[2,576,512]{2,1,0:T(8,128)(2,1)} %bitcast.185), channel_id=1, source_target_pairs={{4,0},{8,4},{12,8},{5,1},{9,5},{13,9},{6,2},{10,6},{14,10},{7,3},{... | collective-permute-start | bytes 3538952 | tf_op jit(solution)/shard_map/ppermute | solution.py:15
  12.6 48.8 %collective-permute-start.2 = (bf16[2,576,512]{2,1,0:T(8,128)(2,1)}, bf16[2,576,512]{2,1,0:T(8,128)(2,1)S(1)}, u32[]{:S(2)}, u32[]{:S(2)}) collective-permute-start(bf16[2,576,512]{2,1,0:T(8,128)(2,1)} %bitcast.187), channel_id=1, source_target_pairs={{0,4},{4,8},{8,12},{1,5},{5,9},{9,13},{2,6},{6,10},{10,14},{3,7},{... | collective-permute-start | bytes 3538952 | tf_op jit(solution)/shard_map/ppermute | solution.py:14
  15.7 48.6 %collective-permute-start.3 = (bf16[2,576,512]{2,1,0:T(8,128)(2,1)}, bf16[2,576,512]{2,1,0:T(8,128)(2,1)S(1)}, u32[]{:S(2)}, u32[]{:S(2)}) collective-permute-start(bf16[2,576,512]{2,1,0:T(8,128)(2,1)} %bitcast.188), channel_id=1, source_target_pairs={{4,0},{8,4},{12,8},{5,1},{9,5},{13,9},{6,2},{10,6},{14,10},{7,3},{... | collective-permute-start | bytes 3538952 | tf_op jit(solution)/shard_map/ppermute | solution.py:15
  21.9 21.0 %copy-start.6 = (bf16[2,2,1,576,1152]{4,3,2,1,0:T(8,128)(2,1)S(1)}, bf16[2,2,1,576,1152]{4,3,2,1,0:T(8,128)(2,1)}, u32[]{:S(2)}) copy-start(bf16[2,2,1,576,1152]{4,3,2,1,0:T(8,128)(2,1)} %param.7) | copy-start | bytes 15925252
  43.8 20.5 %copy-start.1 = (bf16[2,1,576,512]{3,2,1,0:T(8,128)(2,1)S(1)}, bf16[2,1,576,512]{3,2,1,0:T(8,128)(2,1)}, u32[]{:S(2)}) copy-start(bf16[2,1,576,512]{3,2,1,0:T(8,128)(2,1)} %param.6) | copy-start | bytes 3538948
  70.6 2.8 %copy-start.2 = (bf16[1,576,512]{2,1,0:T(8,128)(2,1)}, bf16[1,576,512]{2,1,0:T(8,128)(2,1)S(1)}, u32[]{:S(2)}) copy-start(bf16[1,576,512]{2,1,0:T(8,128)(2,1)S(1)} %fusion.74) | copy-start | bytes 1769476
  71.6 1.9 copy-start.3
  75.7 71.2 %all-gather.2.cloned.1.call-start = ((), (), s32[]{:S(2)}) async-start(), calls=%async_computation.3 | async-start | bytes 2764800 | tf_op jit(solution)/shard_map/all_gather | solution.py:60
  75.9 48.9 %collective-permute-start.8 = (bf16[2,576,512]{2,1,0:T(8,128)(2,1)S(1)}, bf16[2,576,512]{2,1,0:T(8,128)(2,1)}, u32[]{:S(2)}, u32[]{:S(2)}) collective-permute-start(bf16[2,576,512]{2,1,0:T(8,128)(2,1)S(1)} %pad_maximum_fusion.2), channel_id=1, source_target_pairs={{0,4},{4,8},{8,12},{1,5},{5,9},{9,13},{2,6},{6,10},{10,14},{3,7},{... | collective-permute-start | bytes 3538952 | tf_op jit(solution)/shard_map/ppermute | solution.py:14
  79.1 45.7 %collective-permute-start.9 = (bf16[2,576,512]{2,1,0:T(8,128)(2,1)S(1)}, bf16[2,576,512]{2,1,0:T(8,128)(2,1)}, u32[]{:S(2)}, u32[]{:S(2)}) collective-permute-start(bf16[2,576,512]{2,1,0:T(8,128)(2,1)S(1)} %pad_maximum_fusion.2), channel_id=1, source_target_pairs={{4,0},{8,4},{12,8},{5,1},{9,5},{13,9},{6,2},{10,6},{14,10},{7,3},{... | collective-permute-start | bytes 3538952 | tf_op jit(solution)/shard_map/ppermute | solution.py:15
  104.9 7.4 %collective-permute-start.4 = (bf16[144,576]{1,0:T(8,128)(2,1)S(1)}, bf16[144,576]{1,0:T(8,128)(2,1)S(1)}, u32[]{:S(2)}, u32[]{:S(2)}) collective-permute-start(bf16[144,576]{1,0:T(8,128)(2,1)S(1)} %tanh_convert_fusion.1), channel_id=1, source_target_pairs={{0,4},{4,8},{8,12},{1,5},{5,9},{9,13},{2,6},{6,10},{10,14},{3,7},{... | collective-permute-start | bytes 497672 | tf_op jit(solution)/shard_map/ppermute | solution.py:14
  108.0 7.1 %collective-permute-start.5 = (bf16[144,576]{1,0:T(8,128)(2,1)S(1)}, bf16[144,576]{1,0:T(8,128)(2,1)S(1)}, u32[]{:S(2)}, u32[]{:S(2)}) collective-permute-start(bf16[144,576]{1,0:T(8,128)(2,1)S(1)} %tanh_convert_fusion.1), channel_id=1, source_target_pairs={{4,0},{8,4},{12,8},{5,1},{9,5},{13,9},{6,2},{10,6},{14,10},{7,3},{... | collective-permute-start | bytes 497672 | tf_op jit(solution)/shard_map/ppermute | solution.py:15
  116.0 79.3 %reduce-scatter.5.cloned.1.call-start = ((), (), s32[]{:S(2)}) async-start(), calls=%async_computation.4 | async-start | bytes 1843200 | tf_op jit(solution)/shard_map/reduce_scatter | solution.py:53
  119.4 27.6 %collective-permute-start.7 = (bf16[2,576,512]{2,1,0:T(8,128)(2,1)S(1)}, bf16[2,576,512]{2,1,0:T(8,128)(2,1)}, u32[]{:S(2)}, u32[]{:S(2)}) collective-permute-start(bf16[2,576,512]{2,1,0:T(8,128)(2,1)S(1)} %pad_maximum_fusion.1), channel_id=1, source_target_pairs={{4,0},{8,4},{12,8},{5,1},{9,5},{13,9},{6,2},{10,6},{14,10},{7,3},{... | collective-permute-start | bytes 3538952 | tf_op jit(solution)/shard_map/ppermute | solution.py:15
  121.5 31.4 %collective-permute-start.6 = (bf16[2,576,512]{2,1,0:T(8,128)(2,1)S(1)}, bf16[2,576,512]{2,1,0:T(8,128)(2,1)}, u32[]{:S(2)}, u32[]{:S(2)}) collective-permute-start(bf16[2,576,512]{2,1,0:T(8,128)(2,1)S(1)} %pad_maximum_fusion.1), channel_id=1, source_target_pairs={{0,4},{4,8},{8,12},{1,5},{5,9},{9,13},{2,6},{6,10},{10,14},{3,7},{... | collective-permute-start | bytes 3538952 | tf_op jit(solution)/shard_map/ppermute | solution.py:14
  124.9 6.6 %slice-start.1 = ((s8[5308416]{0:T(1024)(128)(4,1)}), s8[4194304]{0:T(1024)(128)(4,1)S(1)}, s32[]{:S(2)}) async-start(s8[5308416]{0:T(1024)(128)(4,1)} %bitcast.196), calls=%async_computation.6 | async-start | bytes 8388608
  129.1 2.4 %slice-start.2 = ((s8[5308416]{0:T(1024)(128)(4,1)}), s8[1114112]{0:T(1024)(128)(4,1)S(1)}, s32[]{:S(2)}) async-start(s8[5308416]{0:T(1024)(128)(4,1)} %bitcast.196), calls=%async_computation.7 | async-start | bytes 2228224
  147.0 3.1 %copy-start = (bf16[3,576,576]{2,1,0:T(8,128)(2,1)S(1)}, bf16[3,576,576]{2,1,0:T(8,128)(2,1)}, u32[]{:S(2)}) copy-start(bf16[3,576,576]{2,1,0:T(8,128)(2,1)} %all-gather.2.cloned.1.call-done) | copy-start | bytes 5971972
  150.1 9.2 %slice-start.3 = ((s8[5308416]{0:T(1024)(128)(4,1)}), s8[4194304]{0:T(1024)(128)(4,1)S(1)}, s32[]{:S(2)}) async-start(s8[5308416]{0:T(1024)(128)(4,1)} %bitcast.198), calls=%async_computation.8 | async-start | bytes 8388608
  152.9 6.4 %slice-start.4 = ((s8[5308416]{0:T(1024)(128)(4,1)}), s8[1114112]{0:T(1024)(128)(4,1)S(1)}, s32[]{:S(2)}) async-start(s8[5308416]{0:T(1024)(128)(4,1)} %bitcast.198), calls=%async_computation.9 | async-start | bytes 2228224
  162.1 1.2 copy-start.7
  162.1 2.0 copy-start.4
  162.1 2.0 copy-start.5
  163.3 0.8 copy-start.9
  167.5 37.7 %copy-start.8 = (bf16[1,576,512]{2,1,0:T(8,128)(2,1)S(1)}, bf16[1,576,512]{2,1,0:T(8,128)(2,1)}, u32[]{:S(2)}) copy-start(bf16[1,576,512]{2,1,0:T(8,128)(2,1)} %copy-done.7) | copy-start | bytes 1769476
  167.5 37.7 %copy-start.10 = (bf16[1,576,512]{2,1,0:T(8,128)(2,1)S(1)}, bf16[1,576,512]{2,1,0:T(8,128)(2,1)}, u32[]{:S(2)}) copy-start(bf16[1,576,512]{2,1,0:T(8,128)(2,1)} %copy-done.9) | copy-start | bytes 1769476
  205.1 2.1 slice-start
Sparse Core Ops, SparseCore 0:
  75.9 27.9 reduce-scatter.2
  116.1 23.8 all-gather.1
  166.5 28.7 reduce-scatter.4

commit v2 on v0

v2 whole, which is shorter than its diff:
```python
import functools
import math

import jax
import jax.numpy as jnp
from jax import lax
from jax.experimental import pallas as pl
from jax.experimental.pallas import tpu as pltpu
from jax.sharding import PartitionSpec as P

LEVELS = 2
F32 = jnp.float32
BF16 = jnp.bfloat16
MESH = pl.DeviceIdType.MESH
PIECES = ((1, 0), (0, 0), (1, 1), (0, 1))


def round_up(value, step):
    return (value + step - 1) // step * step


def migrate(
    lat_count,
    freq_total,
    start_ref,
    slot_ref,
    src_hbm,
    dat_hbm,
    prop_hbm,
    refl_out,
    src_out,
    dat_out,
    prop,
    rows_of,
    ext,
    scat,
    final,
    gram,
    gram_in,
    gram_x,
    refl,
    refl_flat,
    refl_wide,
    own_sem,
    prop_sem,
    out_sem,
    halo_send,
    halo_recv,
    pair_send,
    pair_recv,
    x_send,
    x_recv,
    r_send,
    r_recv,
    z_send,
    z_recv,
):
    tile = src_hbm.shape[1]
    shots = src_hbm.shape[2]
    band = prop_hbm.shape[3]
    reach = ext.shape[3]
    count_x = freq_total // 2
    half = tile // 2
    sub = half // count_x
    part = shots // 2
    lat = lax.axis_index("lat")
    freq = lax.axis_index("freq")
    core = lax.rem(freq, 2)
    chip = freq // 2
    other = 1 - core
    right = lax.rem(lat + 1, lat_count)
    left = lax.rem(lat + lat_count - 1, lat_count)
    has_right = lat < lat_count - 1
    has_left = lat > 0
    sends = (has_right, has_left)
    gets = (has_left, has_right)
    towards = (right, left)
    landing = (0, 2 * tile)
    partner = {"freq": chip * 2 + other}
    fields = (src_hbm, dat_hbm)

    def peer(step):
        return {"freq": lax.rem(chip + step, count_x) * 2 + core}

    def remote(src, dst, send, recv, device):
        return pltpu.make_async_remote_copy(
            src_ref=src, dst_ref=dst, send_sem=send, recv_sem=recv, device_id=device, device_id_type=MESH
        )

    barrier = pltpu.get_barrier_semaphore()
    greeted = [{"lat": left}, {"lat": right}, partner] + [peer(d) for d in range(1, count_x)]
    for device in greeted:
        pl.semaphore_signal(barrier, inc=1, device_id=device, device_id_type=MESH)
    pl.semaphore_wait(barrier, len(greeted))

    def halo(level, piece, way):
        field, block = PIECES[piece]
        cols = pl.ds(block * part, part)
        if level == 0:
            src = fields[field].at[:, :, cols]
        else:
            src = ext.at[1, field, :, pl.ds(tile, tile), cols]
        return remote(
            src,
            ext.at[level, field, :, pl.ds(landing[way], tile), cols],
            halo_send.at[level, piece, way],
            halo_recv.at[level, piece, way],
            {"lat": towards[way]},
        )

    def halo_start(level, piece):
        for way in range(2):
            pl.when(sends[way])(halo(level, piece, way).start)

    def halo_sent(level, piece):
        for way in range(2):
            pl.when(sends[way])(halo(level, piece, way).wait_send)

    def halo_got(level, piece):
        for way in range(2):
            pl.when(gets[way])(halo(level, piece, way).wait_recv)

    halo_start(0, 0)
    halo_start(0, 1)
    props = [pltpu.make_async_copy(prop_hbm.at[v], prop.at[v], prop_sem.at[v]) for v in range(LEVELS)]
    props[0].start()
    owns = [
        pltpu.make_async_copy(fields[f], ext.at[0, f, :, pl.ds(tile, tile)], own_sem.at[f]) for f in range(2)
    ]
    owns[1].start()
    owns[0].start()
    props[1].start()

    slack = reach - 3 * tile
    for f in range(2):
        for c in range(2):
            ext[0, f, c, pl.ds(3 * tile, slack), :] = jnp.zeros((slack, shots), BF16)
            ext[1, f, c, pl.ds(3 * tile, slack), :] = jnp.zeros((slack, shots), BF16)
    for c in range(2):
        scat[c, pl.ds(3 * tile, slack), :] = jnp.zeros((slack, shots), BF16)
    for way in range(2):

        @pl.when(jnp.logical_not(gets[way]))
        def _():
            for level in range(2):
                for f in range(2):
                    for c in range(2):
                        ext[level, f, c, pl.ds(landing[way], tile), :] = jnp.zeros((tile, shots), BF16)
            refl[2 * way] = jnp.zeros(refl.shape[1:], BF16)

    step_rows = 64

    def spread(level):
        shift = start_ref[level]

        @pl.loop(0, tile // step_rows)
        def _(i):
            rows = pl.ds(pl.multiple_of(i * step_rows, step_rows), step_rows)
            gap = jnp.zeros((step_rows, reach - band), F32)

            def moved(c):
                wide = jnp.concatenate([prop[level, c, rows, :].astype(F32), gap], axis=1)
                return pltpu.roll(wide, shift, 1)

            real = moved(0).astype(BF16)
            imag = moved(1)
            rows_of[level, 0, rows, pl.ds(0, reach)] = real
            rows_of[level, 1, rows, pl.ds(reach, reach)] = real
            rows_of[level, 1, rows, pl.ds(0, reach)] = imag.astype(BF16)
            rows_of[level, 0, rows, pl.ds(reach, reach)] = (-imag).astype(BF16)

    def advance(level, window, out, block):
        cols = pl.ds(block * part, part)

        @pl.loop(0, 2)
        def _(c):
            value = jnp.dot(
                rows_of[level, c, :, pl.ds(0, reach)], window[0, :, cols], preferred_element_type=F32
            ) + jnp.dot(
                rows_of[level, c, :, pl.ds(reach, reach)], window[1, :, cols], preferred_element_type=F32
            )
            out[c, :, cols] = value.astype(BF16)

    weight = (slot_ref[0].astype(F32) + 1.0) / (16.0 * freq_total)
    scale = weight * (1.0 / math.sqrt(freq_total * shots))
    nt = (((1,), (1,)), ((), ()))

    def gram_half(level, up, down, h):
        rows = pl.ds(pl.multiple_of(h * half, 32), half)
        value = lax.dot_general(up[0, rows, :], down[0, :, :], nt, preferred_element_type=F32)
        value += lax.dot_general(up[1, rows, :], down[1, :, :], nt, preferred_element_type=F32)
        gram[level, h] = (value * scale).reshape(count_x, sub, tile)

    def pair_copy(level):
        return remote(
            gram.at[level, other], gram_in.at[level], pair_send.at[level], pair_recv.at[level], partner
        )

    def x_copy(level, step):
        return remote(
            gram.at[level, core, lax.rem(chip + step, count_x)],
            gram_x.at[level, step - 1],
            x_send.at[level, 0, step - 1],
            x_recv.at[level, 0, step - 1],
            peer(step),
        )

    def share_copy(level, step):
        mine = refl.at[1 if level == 0 else 3, core, chip]
        return remote(mine, mine, x_send.at[level, 1, step - 1], x_recv.at[level, 1, step - 1], peer(step))

    def swap_copy(slot):
        block = refl.at[slot, core]
        return remote(block, block, r_send.at[slot], r_recv.at[slot], partner)

    def reduce(level, up, down):
        slot = 1 if level == 0 else 3
        gram_half(level, up, down, other)
        pair_copy(level).start()
        gram_half(level, up, down, core)
        pair_copy(level).wait_recv()
        for x in range(count_x):
            gram[level, core, x] = gram[level, core, x] + gram_in[level, x]
        for step in range(1, count_x):
            x_copy(level, step).start()
        total = gram[level, core, chip]
        for step in range(1, count_x):
            x_copy(level, step).wait_recv()
            total = total + gram_x[level, step - 1]
        refl[slot, core, chip] = jnp.tanh(total).astype(BF16)
        for step in range(1, count_x):
            share_copy(level, step).start()
        for step in range(1, count_x):
            share_copy(level, step).wait_recv()
        swap_copy(slot).start()

    def flatten(slot):
        for h in range(2):
            for x in range(count_x):
                rows = pl.ds(h * half + x * sub, sub)
                if sub % 16:
                    refl_wide[rows, :] = refl[slot, h, x].astype(F32)
                else:
                    refl_flat[slot, rows, :] = refl[slot, h, x]
        if sub % 16:
            refl_flat[slot] = refl_wide[...].astype(BF16)

    def z_copy(way):
        return remote(
            refl.at[1, core],
            refl.at[2 * way, core],
            z_send.at[way],
            z_recv.at[way],
            {"lat": towards[way]},
        )

    factor = 1.0 / math.sqrt(tile)

    def scatter(block):
        cols = pl.ds(block * part, part)

        @pl.loop(0, 6)
        def _(i):
            c = i // 3
            place = lax.rem(i, 3)
            rows = pl.ds(pl.multiple_of(place * tile, 64), tile)
            up = ext[1, 0, c, rows, cols]
            add = jnp.dot(refl_flat[place], up, preferred_element_type=F32)
            scat[c, rows, cols] = (up.astype(F32) + add * factor).astype(BF16)

    own = pl.ds(tile, tile)
    props[0].wait()
    spread(0)
    props[1].wait()
    spread(1)
    for copy in owns:
        copy.wait()
    for piece, (field, block) in enumerate(PIECES):
        halo_got(0, piece)
        if piece + 2 < 4:
            halo_sent(0, piece)
            halo_start(0, piece + 2)
        else:
            halo_start(1, piece - 2)
        advance(0, ext.at[0, field], ext.at[1, field, :, own], block)
    halo_start(1, 2)
    halo_start(1, 3)
    reduce(0, ext.at[1, 0, :, own], ext.at[1, 1, :, own])
    for way in range(2):
        pl.when(sends[way])(z_copy(way).start)
    swap_copy(1).wait_recv()
    flatten(1)
    refl_store = pltpu.make_async_copy(refl_flat.at[1], refl_out.at[0], out_sem.at[0])
    refl_store.start()
    halo_got(1, 0)
    advance(1, ext.at[1, 1], final.at[1], 0)
    for way in range(2):

        @pl.when(gets[way])
        def _():
            z_copy(way).wait_recv()
            swap_copy(2 * way).start()

    for way in range(2):

        pl.when(gets[way])(swap_copy(2 * way).wait_recv)
        flatten(2 * way)
    halo_got(1, 1)
    scatter(0)
    advance(1, scat, final.at[0], 0)
    halo_got(1, 2)
    advance(1, ext.at[1, 1], final.at[1], 1)
    dat_store = pltpu.make_async_copy(final.at[1], dat_out, out_sem.at[1])
    dat_store.start()
    halo_got(1, 3)
    scatter(1)
    advance(1, scat, final.at[0], 1)
    reduce(1, final.at[0], final.at[1])
    swap_copy(3).wait_recv()
    flatten(3)
    refl_last = pltpu.make_async_copy(refl_flat.at[3], refl_out.at[1], out_sem.at[2])
    refl_last.start()

    @pl.loop(0, 2)
    def _(c):
        up = final[0, c]
        add = jnp.dot(refl_flat[3], up, preferred_element_type=F32)
        scat[c, pl.ds(0, tile), :] = (up.astype(F32) + add * factor).astype(BF16)

    src_store = pltpu.make_async_copy(scat.at[:, pl.ds(0, tile)], src_out, out_sem.at[3])
    src_store.start()
    for piece in range(4):
        if piece >= 2:
            halo_sent(0, piece)
        halo_sent(1, piece)
    for way in range(2):
        pl.when(sends[way])(z_copy(way).wait_send)
        pl.when(gets[way])(swap_copy(2 * way).wait_send)
    swap_copy(1).wait_send()
    swap_copy(3).wait_send()
    for level in range(2):
        pair_copy(level).wait_send()
        for step in range(1, count_x):
            x_copy(level, step).wait_send()
            share_copy(level, step).wait_send()
    for store in (refl_store, dat_store, refl_last, src_store):
        store.wait()


def per_device(source_field, data_field, propagator, band_start, freq_slot):
    tile = source_field.shape[2]
    shots = source_field.shape[3]
    band = propagator.shape[4]
    lat_count = lax.axis_size("lat")
    freq_total = source_field.shape[1] * lax.axis_size("freq")
    count_x = freq_total // 2
    sub = tile // 2 // count_x
    reach = round_up(3 * tile, 256)
    vmem = pltpu.VMEM
    dma = pltpu.SemaphoreType.DMA
    field = jax.ShapeDtypeStruct((2, tile, shots), BF16)
    refl, src, dat = pl.pallas_call(
        functools.partial(migrate, lat_count, freq_total),
        out_shape=(jax.ShapeDtypeStruct((LEVELS, tile, tile), BF16), field, field),
        in_specs=[pl.BlockSpec(memory_space=pltpu.SMEM)] * 2 + [pl.BlockSpec(memory_space=pl.ANY)] * 3,
        out_specs=[pl.BlockSpec(memory_space=pl.ANY)] * 3,
        scratch_shapes=[
            vmem((LEVELS, 2, tile, band), BF16),
            vmem((LEVELS, 2, tile, 2 * reach), BF16),
            vmem((LEVELS, 2, 2, reach, shots), BF16),
            vmem((2, reach, shots), BF16),
            vmem((2, 2, tile, shots), BF16),
            vmem((LEVELS, 2, count_x, sub, tile), F32),
            vmem((LEVELS, count_x, sub, tile), F32),
            vmem((LEVELS, count_x - 1, sub, tile), F32),
            vmem((4, 2, count_x, sub, tile), BF16),
            vmem((4, tile, tile), BF16),
            vmem((tile if sub % 16 else 8, tile), F32),
            dma((2,)),
            dma((2,)),
            dma((4,)),
            dma((LEVELS, 4, 2)),
            dma((LEVELS, 4, 2)),
            dma((LEVELS,)),
            dma((LEVELS,)),
            dma((LEVELS, 2, count_x - 1)),
            dma((LEVELS, 2, count_x - 1)),
            dma((4,)),
            dma((4,)),
            dma((2,)),
            dma((2,)),
        ],
        compiler_params=pltpu.CompilerParams(
            collective_id=0, has_side_effects=True, vmem_limit_bytes=60 * 1024 * 1024
        ),
    )(
        band_start[:, 0],
        freq_slot,
        source_field[:, 0],
        data_field[:, 0],
        propagator[:, :, 0],
    )
    return refl, src[:, None], dat[:, None]


def solution(mesh):
    return jax.shard_map(
        per_device,
        mesh=mesh,
        in_specs=(
            P("grp", "freq", "lat", None),
            P("grp", "freq", "lat", None),
            P("grp", None, "freq", "lat", None),
            P("grp", "lat"),
            P("freq"),
        ),
        out_specs=(
            P("grp", "lat", None),
            P("grp", "freq", "lat", None),
            P("grp", "freq", "lat", None),
        ),
        check_vma=False,
    )
```

time: 257 us -> 157 us (0.61)
  waiting for transfers between devices: 156 us -> 0 us
  Pallas kernels: 0 us -> 150 us
  matrix products: 27.3 us -> 0 us
  other arithmetic: 23.3 us -> 0 us
  blocking collectives: 17.7 us -> 0 us
  between operations: 18.6 us -> 1.3 us
  starting transfers between devices: 10.8 us -> 0 us
  local copies, waits for them, and re-layouts: 1.51 us -> 5.42 us
    pallas_call x0 -> x1, Pallas kernels: none -> 150 us  [per_device(): pl.pallas_call(functools.partial(migrate, lat_count, freq_total), out_sha...]
    ppermute x4 -> x0, waiting for transfers between devices: 97.2 us -> none  [the longest x2 93.5 us: extended_2(): lax.ppermute(head, axis, [((i + 1) % count, i) for i in range(ends)])]
    reduce_scatter x2 -> x0, waiting for transfers between devices: 59.1 us -> none  [per_device(): lax.psum_scatter(jnp.einsum('f,fxy->xy', weight, per_freq) * norm, 'freq'...]
    dot_general x12 -> x0, matrix products: 27.3 us -> none  [the longest x2 6.33 us: per_device(): jnp.einsum('fxb,nfbs->nfxs', rows_i, window[:, 1], preferred_element_type...]
    all_gather x2 -> x0, blocking collectives: 17.7 us -> none  [per_device(): lax.all_gather(jnp.tanh(share).astype(jnp.bfloat16), 'freq', axis=0, tile...]
    concatenate x2 -> x0, other arithmetic: 13.5 us -> none  [extended_2(): jnp.concatenate([lax.ppermute(tail, axis, [(i, (i + 1) % count) for i in...]
    ppermute x4 -> x0, starting transfers between devices: 10.7 us -> none  [the longest x2 6.5 us: extended_2(): lax.ppermute(tail, axis, [(i, (i + 1) % count) for i in range(ends)])]
    another operation x4 -> x0, other arithmetic: 6.51 us -> none  [the longest x2 5.06 us: per_device(): stacked = jnp.stack([source, record])]
  transfers between devices with their start and end apart: 6 -> 0, of which waited for: 6 -> 0; matrix products, arithmetic and copies ran while one was open for 1% -> 0% of each run, Pallas kernels for 0% -> 0%
where the time goes in v2:
time: 157 us
  Pallas kernels  150 us (96%)
  local copies, waits for them, and re-layouts  5.42 us (3%)
    pallas_call x1, Pallas kernels, per_device(): pl.pallas_call(functools.partial(migrate, lat_count, freq_total), out_sha...  150 us
    unnamed x7, local copies, waits for them, and re-layouts  5.42 us

profile of v2, /device:TPU:11, one launch (start us, length us, event | category | flops | bytes accessed | tf_op | source)
XLA Modules:
  0.0 156.5 jit_solution(1507623525603275687)
XLA Ops:
  1.3 149.8 %shard_map.76 = (bf16[2,576,576]{2,1,0:T(8,128)(2,1)}, bf16[2,576,512]{2,1,0:T(8,128)(2,1)}, bf16[2,576,512]{2,1,0:T(8,128)(2,1)}) custom-call(s32[2]{0:T(128)} %bitcast.15, s32[1]{0:T(128)S(6)} %copy.13.slot_ref, bf16[2,576,512]{2,1,0:T(8,128)(2,1)} %bitcast.13, bf16[2,576,512]{2,1,0:T(8,128)(2,1)} %bitcast.14, bf16[2,2,576,1152]{3,2,1,0:T(8,128)(2,1)} %bitcast.10), custom_call_target="tpu_custom_call" | custom-call | tf_op jit(solution)/shard_map/pallas_call | solution.py:362
  151.1 0.0 copy-start.1
  151.1 2.7 %copy.14 = bf16[2,576,576]{2,1,0:T(8,128)(2,1)} copy(bf16[2,576,576]{2,1,0:T(8,128)(2,1)} %get-tuple-element.15) | data formatting | bytes 2654208
  153.8 0.0 copy-done.1
  153.8 0.0 copy-start
  153.8 1.0 copy.15
  154.8 0.7 copy-done
  155.5 1.0 copy.16
Async XLA Ops:
  151.1 2.7 %copy-start.1 = (bf16[2,576,512]{2,1,0:T(8,128)(2,1)S(1)}, bf16[2,576,512]{2,1,0:T(8,128)(2,1)}, u32[]{:S(2)}) copy-start(bf16[2,576,512]{2,1,0:T(8,128)(2,1)} %get-tuple-element.7) | copy-start | bytes 3538948
  153.8 1.7 %copy-start = (bf16[2,576,512]{2,1,0:T(8,128)(2,1)S(1)}, bf16[2,576,512]{2,1,0:T(8,128)(2,1)}, u32[]{:S(2)}) copy-start(bf16[2,576,512]{2,1,0:T(8,128)(2,1)} %get-tuple-element.8) | copy-start | bytes 3538948

commit v3 on v2

--- a/solution.py
+++ b/solution.py
@@ -12,7 +12,7 @@
 F32 = jnp.float32
 BF16 = jnp.bfloat16
 MESH = pl.DeviceIdType.MESH
-PIECES = ((1, 0), (0, 0), (1, 1), (0, 1))
+PIECES = ((1, 0), (0, 0), (0, 1), (1, 1))
 
 
 def round_up(value, step):
@@ -37,6 +37,7 @@
     final,
     gram,
     gram_in,
+    gram_out,
     gram_x,
     refl,
     refl_flat,
@@ -50,8 +51,10 @@
     pair_recv,
     x_send,
     x_recv,
-    r_send,
-    r_recv,
+    share_send,
+    share_recv,
+    swap_send,
+    swap_recv,
     z_send,
     z_recv,
 ):
@@ -185,54 +188,82 @@
     scale = weight * (1.0 / math.sqrt(freq_total * shots))
     nt = (((1,), (1,)), ((), ()))
 
-    def gram_half(level, up, down, h):
+    def gram_half(level, up, down, h, block):
         rows = pl.ds(pl.multiple_of(h * half, 32), half)
-        value = lax.dot_general(up[0, rows, :], down[0, :, :], nt, preferred_element_type=F32)
-        value += lax.dot_general(up[1, rows, :], down[1, :, :], nt, preferred_element_type=F32)
-        gram[level, h] = (value * scale).reshape(count_x, sub, tile)
-
-    def pair_copy(level):
+        cols = pl.ds(block * part, part)
+        value = lax.dot_general(up[0, rows, cols], down[0, :, cols], nt, preferred_element_type=F32)
+        value += lax.dot_general(up[1, rows, cols], down[1, :, cols], nt, preferred_element_type=F32)
+        value = (value * scale).reshape(count_x, sub, tile)
+        if block:
+            value = value + gram[level, h]
+        gram[level, h] = value
+
+    def ahead(step):
+        return lax.rem(chip + step, count_x)
+
+    def behind(step):
+        return lax.rem(chip + count_x - step, count_x)
+
+    def pair_copy(level, step):
         return remote(
-            gram.at[level, other], gram_in.at[level], pair_send.at[level], pair_recv.at[level], partner
+            gram.at[level, other, ahead(step)],
+            gram_in.at[level, ahead(step)],
+            pair_send.at[level, step],
+            pair_recv.at[level, step],
+            partner,
         )
 
     def x_copy(level, step):
         return remote(
-            gram.at[level, core, lax.rem(chip + step, count_x)],
+            gram_out.at[level, step - 1],
             gram_x.at[level, step - 1],
-            x_send.at[level, 0, step - 1],
-            x_recv.at[level, 0, step - 1],
+            x_send.at[level, step - 1],
+            x_recv.at[level, step - 1],
             peer(step),
         )
 
-    def share_copy(level, step):
-        mine = refl.at[1 if level == 0 else 3, core, chip]
-        return remote(mine, mine, x_send.at[level, 1, step - 1], x_recv.at[level, 1, step - 1], peer(step))
-
-    def swap_copy(slot):
-        block = refl.at[slot, core]
-        return remote(block, block, r_send.at[slot], r_recv.at[slot], partner)
-
-    def reduce(level, up, down):
-        slot = 1 if level == 0 else 3
-        gram_half(level, up, down, other)
-        pair_copy(level).start()
-        gram_half(level, up, down, core)
-        pair_copy(level).wait_recv()
-        for x in range(count_x):
-            gram[level, core, x] = gram[level, core, x] + gram_in[level, x]
+    def share_copy(slot, step):
+        mine = refl.at[slot, core, chip]
+        return remote(mine, mine, share_send.at[slot, step - 1], share_recv.at[slot, step - 1], peer(step))
+
+    def swap_copy(slot, step):
+        block = refl.at[slot, core, behind(step)]
+        return remote(block, block, swap_send.at[slot, step], swap_recv.at[slot, step], partner)
+
+    def share_start(slot):
         for step in range(1, count_x):
-            x_copy(level, step).start()
-        total = gram[level, core, chip]
+            share_copy(slot, step).start()
+        swap_copy(slot, 0).start()
+
+    def share_finish(slot):
+        for step in range(1, count_x):
+            share_copy(slot, step).wait_recv()
+            swap_copy(slot, step).start()
+        for step in range(count_x):
+            swap_copy(slot, step).wait_recv()
+
+    def share_sent(slot):
+        for step in range(1, count_x):
+            share_copy(slot, step).wait_send()
+        for step in range(count_x):
+            swap_copy(slot, step).wait_send()
+
+    def reduce(level, slot, up, down):
+        order = list(range(1, count_x)) + [0]
+        gram_half(level, up, down, other, 1)
+        for step in order:
+            pair_copy(level, step).start()
+        gram_half(level, up, down, core, 1)
+        for step in order:
+            pair_copy(level, step).wait_recv()
+            total = gram[level, core, ahead(step)] + gram_in[level, ahead(step)]
+            if step:
+                gram_out[level, step - 1] = total.astype(BF16)
+                x_copy(level, step).start()
         for step in range(1, count_x):
             x_copy(level, step).wait_recv()
-            total = total + gram_x[level, step - 1]
+            total = total + gram_x[level, step - 1].astype(F32)
         refl[slot, core, chip] = jnp.tanh(total).astype(BF16)
-        for step in range(1, count_x):
-            share_copy(level, step).start()
-        for step in range(1, count_x):
-            share_copy(level, step).wait_recv()
-        swap_copy(slot).start()
 
     def flatten(slot):
         for h in range(2):
@@ -247,8 +278,8 @@
 
     def z_copy(way):
         return remote(
-            refl.at[1, core],
-            refl.at[2 * way, core],
+            refl.at[1, core, chip],
+            refl.at[2 * way, core, chip],
             z_send.at[way],
             z_recv.at[way],
             {"lat": towards[way]},
@@ -283,67 +314,94 @@
         else:
             halo_start(1, piece - 2)
         advance(0, ext.at[0, field], ext.at[1, field, :, own], block)
+        if piece == 1:
+            for h in range(2):
+                gram_half(0, ext.at[1, 0, :, own], ext.at[1, 1, :, own], h, 0)
     halo_start(1, 2)
-    halo_start(1, 3)
-    reduce(0, ext.at[1, 0, :, own], ext.at[1, 1, :, own])
+    reduce(0, 1, ext.at[1, 0, :, own], ext.at[1, 1, :, own])
     for way in range(2):
         pl.when(sends[way])(z_copy(way).start)
-    swap_copy(1).wait_recv()
+    share_start(1)
+    halo_start(1, 3)
+    share_finish(1)
     flatten(1)
     refl_store = pltpu.make_async_copy(refl_flat.at[1], refl_out.at[0], out_sem.at[0])
     refl_store.start()
+    for way in range(2):
+
+        @pl.when(gets[way])
+        def _():
+            z_copy(way).wait_recv()
+            share_start(2 * way)
+
     halo_got(1, 0)
     advance(1, ext.at[1, 1], final.at[1], 0)
     for way in range(2):
-
-        @pl.when(gets[way])
-        def _():
-            z_copy(way).wait_recv()
-            swap_copy(2 * way).start()
-
-    for way in range(2):
-
-        pl.when(gets[way])(swap_copy(2 * way).wait_recv)
+        pl.when(gets[way])(functools.partial(share_finish, 2 * way))
         flatten(2 * way)
     halo_got(1, 1)
     scatter(0)
     advance(1, scat, final.at[0], 0)
+    for h in range(2):
+        gram_half(1, final.at[0], final.at[1], h, 0)
     halo_got(1, 2)
+    scatter(1)
+    advance(1, scat, final.at[0], 1)
+    src_store = pltpu.make_async_copy(final.at[0], src_out, out_sem.at[3])
+    src_store.start()
+    halo_got(1, 3)
     advance(1, ext.at[1, 1], final.at[1], 1)
     dat_store = pltpu.make_async_copy(final.at[1], dat_out, out_sem.at[1])
+    reduce(1, 3, final.at[0], final.at[1])
+    share_start(3)
     dat_store.start()
-    halo_got(1, 3)
-    scatter(1)
-    advance(1, scat, final.at[0], 1)
-    reduce(1, final.at[0], final.at[1])
-    swap_copy(3).wait_recv()
+    share_finish(3)
     flatten(3)
     refl_last = pltpu.make_async_copy(refl_flat.at[3], refl_out.at[1], out_sem.at[2])
     refl_last.start()
-
-    @pl.loop(0, 2)
-    def _(c):
-        up = final[0, c]
-        add = jnp.dot(refl_flat[3], up, preferred_element_type=F32)
-        scat[c, pl.ds(0, tile), :] = (up.astype(F32) + add * factor).astype(BF16)
-
-    src_store = pltpu.make_async_copy(scat.at[:, pl.ds(0, tile)], src_out, out_sem.at[3])
-    src_store.start()
     for piece in range(4):
         if piece >= 2:
             halo_sent(0, piece)
         halo_sent(1, piece)
     for way in range(2):
         pl.when(sends[way])(z_copy(way).wait_send)
-        pl.when(gets[way])(swap_copy(2 * way).wait_send)
-    swap_copy(1).wait_send()
-    swap_copy(3).wait_send()
+        pl.when(gets[way])(functools.partial(share_sent, 2 * way))
+    share_sent(1)
+    share_sent(3)
     for level in range(2):
-        pair_copy(level).wait_send()
+        for step in range(count_x):
+            pair_copy(level, step).wait_send()
         for step in range(1, count_x):
             x_copy(level, step).wait_send()
-            share_copy(level, step).wait_send()
     for store in (refl_store, dat_store, refl_last, src_store):
+        store.wait()
+
+
+def finish(refl_in, up_in, dat_in, refl_out, src_out, dat_out, refl, up, dat, done, in_sem, out_sem):
+    tile = up_in.shape[1]
+    factor = 1.0 / math.sqrt(tile)
+    last = LEVELS - 1
+    moves = [(refl_in.at[v], refl.at[v], refl_out.at[v]) for v in range(last, -1, -1)]
+    moves += [(dat_in.at[c], dat.at[c], dat_out.at[c]) for c in range(2)]
+    fetch = [pltpu.make_async_copy(up_in.at[c], up.at[c], in_sem.at[c]) for c in range(2)]
+    loads = [pltpu.make_async_copy(m[0], m[1], in_sem.at[2 + i]) for i, m in enumerate(moves)]
+    stores = [pltpu.make_async_copy(m[1], m[2], out_sem.at[2 + i]) for i, m in enumerate(moves)]
+    for load in [loads[0]] + fetch + loads[1:]:
+        load.start()
+    loads[0].wait()
+    stores[0].start()
+    for c in range(2):
+        fetch[c].wait()
+        field = up[c]
+        add = jnp.dot(refl[last], field, preferred_element_type=F32)
+        done[c] = (field.astype(F32) + add * factor).astype(BF16)
+        store = pltpu.make_async_copy(done.at[c], src_out.at[c], out_sem.at[c])
+        store.start()
+        stores.append(store)
+        for i in range(1 + c, len(moves), 2):
+            loads[i].wait()
+            stores[i].start()
+    for store in stores:
         store.wait()
 
 
@@ -359,9 +417,10 @@
     vmem = pltpu.VMEM
     dma = pltpu.SemaphoreType.DMA
     field = jax.ShapeDtypeStruct((2, tile, shots), BF16)
-    refl, src, dat = pl.pallas_call(
+    whole = jax.ShapeDtypeStruct((LEVELS, tile, tile), BF16)
+    refl, up, dat = pl.pallas_call(
         functools.partial(migrate, lat_count, freq_total),
-        out_shape=(jax.ShapeDtypeStruct((LEVELS, tile, tile), BF16), field, field),
+        out_shape=(whole, field, field),
         in_specs=[pl.BlockSpec(memory_space=pltpu.SMEM)] * 2 + [pl.BlockSpec(memory_space=pl.ANY)] * 3,
         out_specs=[pl.BlockSpec(memory_space=pl.ANY)] * 3,
         scratch_shapes=[
@@ -372,7 +431,8 @@
             vmem((2, 2, tile, shots), BF16),
             vmem((LEVELS, 2, count_x, sub, tile), F32),
             vmem((LEVELS, count_x, sub, tile), F32),
-            vmem((LEVELS, count_x - 1, sub, tile), F32),
+            vmem((LEVELS, count_x - 1, sub, tile), BF16),
+            vmem((LEVELS, count_x - 1, sub, tile), BF16),
             vmem((4, 2, count_x, sub, tile), BF16),
             vmem((4, tile, tile), BF16),
             vmem((tile if sub % 16 else 8, tile), F32),
@@ -381,12 +441,14 @@
             dma((4,)),
             dma((LEVELS, 4, 2)),
             dma((LEVELS, 4, 2)),
-            dma((LEVELS,)),
-            dma((LEVELS,)),
-            dma((LEVELS, 2, count_x - 1)),
-            dma((LEVELS, 2, count_x - 1)),
-            dma((4,)),
-            dma((4,)),
+            dma((LEVELS, count_x)),
+            dma((LEVELS, count_x)),
+            dma((LEVELS, count_x - 1)),
+            dma((LEVELS, count_x - 1)),
+            dma((4, count_x - 1)),
+            dma((4, count_x - 1)),
+            dma((4, count_x)),
+            dma((4, count_x)),
             dma((2,)),
             dma((2,)),
         ],
@@ -400,6 +462,20 @@
         data_field[:, 0],
         propagator[:, :, 0],
     )
+    refl, src, dat = pl.pallas_call(
+        finish,
+        out_shape=(whole, field, field),
+        in_specs=[pl.BlockSpec(memory_space=pl.ANY)] * 3,
+        out_specs=[pl.BlockSpec(memory_space=pl.ANY)] * 3,
+        scratch_shapes=[
+            vmem((LEVELS, tile, tile), BF16),
+            vmem((2, tile, shots), BF16),
+            vmem((2, tile, shots), BF16),
+            vmem((2, tile, shots), BF16),
+            dma((4 + LEVELS,)),
+            dma((4 + LEVELS,)),
+        ],
+    )(refl, up, dat)
     return refl, src[:, None], dat[:, None]
 
 

time: 157 us -> 142 us (0.904)
  Pallas kernels: 150 us -> 139 us
  local copies, waits for them, and re-layouts: 5.42 us -> 0 us
    pallas_call x1, Pallas kernels: 150 us -> 136 us  [per_device(): pl.pallas_call(functools.partial(migrate, lat_count, freq_total), out_sha...]
    unnamed x7 -> x0, local copies, waits for them, and re-layouts: 5.42 us -> none
    pallas_call x0 -> x1, Pallas kernels: none -> 3.84 us  [per_device(): pl.pallas_call(finish, out_shape=(whole, field, field), in_specs=[pl.Bloc...]
where the time goes in v3:
time: 142 us; the launch traced here: 141 us
  Pallas kernels  139 us (98%)
    pallas_call x1, Pallas kernels, per_device(): pl.pallas_call(functools.partial(migrate, lat_count, freq_total), out_sha...  136 us
    pallas_call x1, Pallas kernels, per_device(): pl.pallas_call(finish, out_shape=(whole, field, field), in_specs=[pl.Bloc...  3.84 us

profile of v3, /device:TPU:11, one launch (start us, length us, event | category | flops | bytes accessed | tf_op | source)
XLA Modules:
  0.0 140.7 jit_solution(2386116313923179309)
XLA Ops:
  1.3 135.6 %shard_map.76 = (bf16[2,576,576]{2,1,0:T(8,128)(2,1)}, bf16[2,576,512]{2,1,0:T(8,128)(2,1)}, bf16[2,576,512]{2,1,0:T(8,128)(2,1)}) custom-call(s32[2]{0:T(128)} %bitcast.13, s32[1]{0:T(128)S(6)} %copy.10.slot_ref, bf16[2,576,512]{2,1,0:T(8,128)(2,1)} %bitcast.11, bf16[2,576,512]{2,1,0:T(8,128)(2,1)} %bitcast.12, bf16[2,2,576,1152]{3,2,1,0:T(8,128)(2,1)} %bitcast.10), custom_call_target="tpu_custom_call" | custom-call | tf_op jit(solution)/shard_map/pallas_call | solution.py:421
  136.9 3.8 %shard_map.77 = (bf16[2,576,576]{2,1,0:T(8,128)(2,1)}, bf16[2,576,512]{2,1,0:T(8,128)(2,1)}, bf16[2,576,512]{2,1,0:T(8,128)(2,1)}) custom-call(bf16[2,576,576]{2,1,0:T(8,128)(2,1)} %get-tuple-element.9.refl_in, bf16[2,576,512]{2,1,0:T(8,128)(2,1)} %get-tuple-element.10.up_in, bf16[2,576,512]{2,1,0:T(8,128)(2,1)} %get-tuple-element.11.dat_in), custom_call_target="tpu_custom_call" | custom-call | tf_op jit(solution)/shard_map/pallas_call | solution.py:465

commit v4 on v3

--- a/solution.py
+++ b/solution.py
@@ -317,11 +317,11 @@
         if piece == 1:
             for h in range(2):
                 gram_half(0, ext.at[1, 0, :, own], ext.at[1, 1, :, own], h, 0)
-    halo_start(1, 2)
     reduce(0, 1, ext.at[1, 0, :, own], ext.at[1, 1, :, own])
     for way in range(2):
         pl.when(sends[way])(z_copy(way).start)
     share_start(1)
+    halo_start(1, 2)
     halo_start(1, 3)
     share_finish(1)
     flatten(1)

time: 142 us -> 135 us (0.951)
  Pallas kernels: 139 us -> 133 us
    pallas_call x1, Pallas kernels: 136 us -> 129 us  [per_device(): pl.pallas_call(functools.partial(migrate, lat_count, freq_total), out_sha...]
where the time goes in v4:
time: 135 us
  Pallas kernels  133 us (99%)
    pallas_call x1, Pallas kernels, per_device(): pl.pallas_call(functools.partial(migrate, lat_count, freq_total), out_sha...  129 us
    pallas_call x1, Pallas kernels, per_device(): pl.pallas_call(finish, out_shape=(whole, field, field), in_specs=[pl.Bloc...  3.84 us

profile of v4, /device:TPU:11, one launch (start us, length us, event | category | flops | bytes accessed | tf_op | source)
XLA Modules:
  0.0 134.5 jit_solution(8504896454244595637)
XLA Ops:
  1.3 129.4 %shard_map.76 = (bf16[2,576,576]{2,1,0:T(8,128)(2,1)}, bf16[2,576,512]{2,1,0:T(8,128)(2,1)}, bf16[2,576,512]{2,1,0:T(8,128)(2,1)}) custom-call(s32[2]{0:T(128)} %bitcast.13, s32[1]{0:T(128)S(6)} %copy.10.slot_ref, bf16[2,576,512]{2,1,0:T(8,128)(2,1)} %bitcast.11, bf16[2,576,512]{2,1,0:T(8,128)(2,1)} %bitcast.12, bf16[2,2,576,1152]{3,2,1,0:T(8,128)(2,1)} %bitcast.10), custom_call_target="tpu_custom_call" | custom-call | tf_op jit(solution)/shard_map/pallas_call | solution.py:421
  130.7 3.8 %shard_map.77 = (bf16[2,576,576]{2,1,0:T(8,128)(2,1)}, bf16[2,576,512]{2,1,0:T(8,128)(2,1)}, bf16[2,576,512]{2,1,0:T(8,128)(2,1)}) custom-call(bf16[2,576,576]{2,1,0:T(8,128)(2,1)} %get-tuple-element.9.refl_in, bf16[2,576,512]{2,1,0:T(8,128)(2,1)} %get-tuple-element.10.up_in, bf16[2,576,512]{2,1,0:T(8,128)(2,1)} %get-tuple-element.11.dat_in), custom_call_target="tpu_custom_call" | custom-call | tf_op jit(solution)/shard_map/pallas_call | solution.py:465
